TPU v7x, 32 devices: a whole 2x2x4 slice. The times are simulated.
32 devices in a mesh: ctx: 4 (over z), section: 2 (over x), mp: 4 (over y, core).
Axes of the slice: x: 2, y: 2, z: 4, core: 2. Of those that a mesh axis runs over, the one named last changes fastest.
Arguments:
- patches: bfloat16 [2, 768, 3200], P(None, ('ctx', 'mp')), may hold values from -16 to 16
- carried: bfloat16 [768, 3200], P(('ctx', 'mp')), may hold values from -16 to 16
- norm_gain: float32 [2, 3200], P('section'), may hold values from 0.1 to 1.9
- q_gain: float32 [2, 128], P('section'), may hold values from 1.5 to 2.5
- k_gain: float32 [2, 128], P('section'), may hold values from 1.5 to 2.5
- q_weight: bfloat16 [2, 3200, 2048], P('section', None, 'mp'), may hold values from -0.109375 to 0.109375
- k_weight: bfloat16 [2, 3200, 2048], P('section', None, 'mp'), may hold values from -0.109375 to 0.109375
- v_weight: bfloat16 [2, 3200, 2048], P('section', None, 'mp'), may hold values from -0.109375 to 0.109375
- o_weight: bfloat16 [2, 2048, 3200], P('section', 'mp', 'ctx'), may hold values from -0.125 to 0.125
Outputs:
- section_outputs: bfloat16 [2, 2, 768, 3200], P('section', None, ('ctx', 'mp'))
All inputs are finite; a program needn't handle non-finite values.
Results may differ from a plain program's by a relative error of at most 0.0063.
Values may be sent and summed in bfloat16 or wider, within the bound.
A program may use at most 128 MiB of HBM per device.

v0:
```python
import math
import jax
import jax.numpy as jnp
from jax import lax
from jax.sharding import PartitionSpec as P

epsilon = 1e-06


def shifted(value, axis, steps):
    count = lax.axis_size(axis)
    leading, last = (max(0, -steps), min(count, count - steps))
    return lax.ppermute(value, axis, [(source, source + steps) for source in range(leading, last)])


def rms_scaled(values, gain):
    return values * lax.rsqrt(jnp.mean(values * values, axis=-1, keepdims=True) + epsilon) * gain


def per_device(patches, carried, norm_gain, q_gain, k_gain, q_weight, k_weight, v_weight, o_weight):
    micro_count = patches.shape[0]
    head_dim = q_gain.shape[1]
    head_count = q_weight.shape[2] // head_dim
    columns = head_count * head_dim
    score_scale = 1.0 / math.sqrt(head_dim)
    section_index = lax.axis_index("section")
    layer_gain = norm_gain[0]
    query_gain = q_gain[0]
    key_gain = k_gain[0]
    incoming = carried
    results = []
    for micro_step in range(micro_count):
        layer_input = jnp.where(section_index == 0, patches[micro_step], incoming)
        residual = layer_input.astype(jnp.float32)
        normed = rms_scaled(residual, layer_gain).astype(jnp.bfloat16)
        project_segment = lax.all_gather(normed, "mp", axis=0, tiled=True)
        project_count = project_segment.shape[0]
        raw_query = jnp.dot(project_segment, q_weight[0], preferred_element_type=jnp.float32)
        raw_key = jnp.dot(project_segment, k_weight[0], preferred_element_type=jnp.float32)
        raw_value = jnp.dot(project_segment, v_weight[0], preferred_element_type=jnp.float32)
        query_rows = rms_scaled(
            raw_query.reshape(project_count, head_count, head_dim), query_gain
        ).reshape(project_count, columns)
        key_rows = rms_scaled(
            raw_key.reshape(project_count, head_count, head_dim), key_gain
        ).reshape(project_count, columns)
        projected = jnp.stack(
            (
                query_rows.astype(jnp.bfloat16),
                key_rows.astype(jnp.bfloat16),
                raw_value.astype(jnp.bfloat16),
            ),
            0,
        )
        block_count = projected.shape[1]
        attend_queries = projected[0].reshape(block_count, head_count, head_dim)
        key_block = lax.all_gather(projected[1], "ctx", axis=0, tiled=True)
        count = key_block.shape[0]
        scores = (
            jnp.einsum(
                "qhd,khd->qhk",
                attend_queries,
                key_block.reshape(count, head_count, head_dim),
                preferred_element_type=jnp.float32,
            )
            * score_scale
        )
        probs = jnp.exp(scores)
        totals = jnp.sum(probs, axis=2)
        weighted = jnp.einsum(
            "qhk,khd->qhd",
            probs.astype(jnp.bfloat16),
            lax.all_gather(projected[2], "ctx", axis=0, tiled=True).reshape(
                count, head_count, head_dim
            ),
            preferred_element_type=jnp.float32,
        )
        attended = (
            (weighted / totals[:, :, None]).reshape(block_count, columns).astype(jnp.bfloat16)
        )
        partial_value = jnp.dot(
            attended,
            lax.all_gather(o_weight[0], "ctx", axis=1, tiled=True),
            preferred_element_type=jnp.float32,
        )
        summed = lax.psum_scatter(partial_value, "mp", scatter_dimension=0, tiled=True)
        layer_out = (residual + summed).astype(jnp.bfloat16)
        results.append(layer_out)
        if micro_step + 1 < micro_count:
            incoming = shifted(layer_out, "section", 1)
    return jnp.stack(results)[None]


def solution(mesh):
    in_specs = (
        P(None, ("ctx", "mp"), None),
        P(("ctx", "mp"), None),
        P("section", None),
        P("section", None),
        P("section", None),
        P("section", None, "mp"),
        P("section", None, "mp"),
        P("section", None, "mp"),
        P("section", "mp", "ctx"),
    )
    out_specs = P("section", None, ("ctx", "mp"), None)
    return jax.shard_map(
        per_device, mesh=mesh, in_specs=in_specs, out_specs=out_specs, check_vma=False
    )
```

profile of v0, /device:TPU:0, one launch (start us, length us, event | category | flops | bytes accessed | tf_op | source)
XLA Modules:
  0.0 286.1 jit_solution(7352324095041157773)
XLA Ops:
  6.5 2.0 fusion.34
  8.6 0.8 reduce
  9.4 1.8 fusion.36
  11.2 0.0 all-gather.5.cloned.1.call-update
  11.2 0.0 all-gather.9.cloned.1.call-start
  11.3 0.7 all-gather.9.cloned.1.call-update
  12.0 0.0 reduce-scatter.3.cloned.1.call-start
  12.0 5.6 %copy.32 = bf16[512,3200]{1,0:T(8,128)(2,1)} copy(bf16[512,3200]{0,1:T(8,128)(2,1)} %bitcast.129) | data formatting | bytes 6553600 | tf_op jit(solution)/shard_map/dot_general | solution.py:39
  17.6 5.8 %copy.33 = bf16[512,3200]{1,0:T(8,128)(2,1)} copy(bf16[512,3200]{0,1:T(8,128)(2,1)} %bitcast.130) | data formatting | bytes 6553600 | tf_op jit(solution)/shard_map/dot_general | solution.py:38
  23.5 8.4 %all-gather.5.cloned.1.call-done = bf16[192,3200]{1,0:T(8,128)(2,1)} async-done(((bf16[48,3200]{1,0:T(8,128)(2,1)}), bf16[192,3200]{1,0:T(8,128)(2,1)}) %all-gather.5.cloned.1.call-update) | async-done | bytes 1228816 | tf_op jit(solution)/shard_map/all_gather | solution.py:36
  31.9 3.7 %multiply_reduce_fusion.3 = (f32[192,4]{0,1:T(4,128)S(1)}, f32[192,4,128]{2,0,1:T(8,128)S(1)}) fusion(bf16[4,128,3200]{2,1,0:T(8,128)(2,1)} %bitcast.131, bf16[192,3200]{1,0:T(8,128)(2,1)} %all-gather.5.cloned.1.call-done), kind=kOutput, calls=%fused_computation.60 | convolution fusion | flops 629341440 | bytes 4901888 | tf_op jit(solution)/shard_map/dot_general | solution.py:39
  35.6 0.2 copy_bitcast_fusion.1
  35.8 28.3 %all_gather.24 = bf16[768,512]{1,0:T(8,128)(2,1)} all-gather(bf16[192,512]{1,0:T(8,128)(2,1)S(1)} %copy_bitcast_fusion.1), channel_id=1, replica_groups=mesh['ctx'=4,'section'=2,'mp'=4] {'ctx'}, dimensions={0}, use_global_device_ids=true | all-gather | bytes 983040 | tf_op jit(solution)/shard_map/all_gather | solution.py:57
  64.1 2.3 copy.18
  66.4 3.8 %multiply_reduce_fusion.2 = (f32[192,4]{0,1:T(4,128)S(1)}, f32[192,4,128]{2,0,1:T(8,128)S(1)}) fusion(bf16[4,128,3200]{2,1,0:T(8,128)(2,1)} %bitcast.133, bf16[192,3200]{1,0:T(8,128)(2,1)} %all-gather.5.cloned.1.call-done), kind=kOutput, calls=%fused_computation.58 | convolution fusion | flops 629341440 | bytes 4901888 | tf_op jit(solution)/shard_map/dot_general | solution.py:38
  70.3 0.8 fusion.22
  71.1 30.4 %all_gather.23 = bf16[768,512]{1,0:T(8,128)(2,1)S(1)} all-gather(bf16[192,512]{1,0:T(8,128)(2,1)S(1)} %fusion.22), channel_id=1, replica_groups=mesh['ctx'=4,'section'=2,'mp'=4] {'ctx'}, dimensions={0}, use_global_device_ids=true | all-gather | bytes 983040 | tf_op jit(solution)/shard_map/all_gather | solution.py:73
  101.5 0.7 bitcast_reduce_fusion.1
  102.2 0.5 fusion.28
  102.7 16.9 %all-gather.9.cloned.1.call-done = bf16[1,512,3200]{1,2,0:T(8,128)(2,1)} async-done(((bf16[1,512,800]{1,2,0:T(8,128)(2,1)}), bf16[1,512,3200]{1,2,0:T(8,128)(2,1)}) %all-gather.9.cloned.1.call-update) | async-done | bytes 3276816 | tf_op jit(solution)/shard_map/all_gather | solution.py:83
  119.7 4.6 %fusion.2 = f32[192,3200]{1,0:T(8,128)} fusion(bf16[1,512,3200]{1,2,0:T(8,128)(2,1)} %all-gather.9.cloned.1.call-done, bf16[4,24,8,128]{3,2,1,0:T(8,128)(2,1)S(1)} %fusion.28), kind=kOutput, calls=%fused_computation.2 | convolution fusion | flops 629145600 | bytes 5931008 | tf_op jit(solution)/shard_map/dot_general | solution.py:81
  124.3 0.0 reduce-scatter.3.cloned.1.call-update
  124.3 0.0 all-gather.7.cloned.1.call-start
  124.3 32.9 %reduce-scatter.3.cloned.1.call-done = f32[48,3200]{1,0:T(8,128)} async-done(((f32[192,3200]{1,0:T(8,128)}), f32[48,3200]{1,0:T(8,128)}) %reduce-scatter.3.cloned.1.call-update) | async-done | bytes 614416 | tf_op jit(solution)/shard_map/reduce_scatter | solution.py:86
  157.2 1.2 fusion.37
  158.4 3.4 %collective-permute-start = (bf16[48,3200]{1,0:T(8,128)(2,1)S(1)}, bf16[48,3200]{1,0:T(8,128)(2,1)S(1)}, u32[]{:S(2)}, u32[]{:S(2)}) collective-permute-start(bf16[48,3200]{1,0:T(8,128)(2,1)S(1)} %fusion.37), channel_id=1, source_target_pairs={{0,4},{1,5},{2,6},{3,7},{8,12},{9,13},{10,14},{11,15},{16,20},{17,... | collective-permute-start | bytes 921608 | tf_op jit(solution)/shard_map/ppermute | solution.py:13
  161.8 6.5 %collective-permute-done = bf16[48,3200]{1,0:T(8,128)(2,1)S(1)} collective-permute-done((bf16[48,3200]{1,0:T(8,128)(2,1)S(1)}, bf16[48,3200]{1,0:T(8,128)(2,1)S(1)}, u32[]{:S(2)}, u32[]{:S(2)}) %collective-permute-start) | collective-permute-done | bytes 307232 | tf_op jit(solution)/shard_map/ppermute | solution.py:13
  168.3 1.2 fusion.38
  169.5 0.7 copy-done.5
  170.2 0.9 fusion.40
  171.1 0.0 all-gather.7.cloned.1.call-update
  171.1 0.0 reduce-scatter.5.cloned.1.call-start
  171.1 18.8 %all-gather.7.cloned.1.call-done = bf16[192,3200]{1,0:T(8,128)(2,1)} async-done(((bf16[48,3200]{1,0:T(8,128)(2,1)}), bf16[192,3200]{1,0:T(8,128)(2,1)}) %all-gather.7.cloned.1.call-update) | async-done | bytes 1228816 | tf_op jit(solution)/shard_map/all_gather | solution.py:36
  190.0 4.4 %multiply_reduce_fusion = (f32[192,4]{0,1:T(4,128)S(1)}, f32[192,4,128]{2,0,1:T(8,128)}) fusion(bf16[4,128,3200]{2,1,0:T(8,128)(2,1)} %bitcast.134, bf16[192,3200]{1,0:T(8,128)(2,1)} %all-gather.7.cloned.1.call-done), kind=kOutput, calls=%fused_computation.54 | convolution fusion | flops 629341440 | bytes 4901888 | tf_op jit(solution)/shard_map/dot_general | solution.py:38
  194.4 1.4 multiply_reduce_fusion.1
  195.8 0.2 copy_bitcast_fusion
  196.0 19.9 %all_gather.28 = bf16[768,512]{1,0:T(8,128)(2,1)} all-gather(bf16[192,512]{1,0:T(8,128)(2,1)S(1)} %copy_bitcast_fusion), channel_id=1, replica_groups=mesh['ctx'=4,'section'=2,'mp'=4] {'ctx'}, dimensions={0}, use_global_device_ids=true | all-gather | bytes 983040 | tf_op jit(solution)/shard_map/all_gather | solution.py:57
  216.0 2.3 copy.25
  218.3 2.2 fusion.25
  220.5 18.2 %all_gather.27 = bf16[768,512]{1,0:T(8,128)(2,1)S(1)} all-gather(bf16[192,512]{1,0:T(8,128)(2,1)S(1)} %fusion.25), channel_id=1, replica_groups=mesh['ctx'=4,'section'=2,'mp'=4] {'ctx'}, dimensions={0}, use_global_device_ids=true | all-gather | bytes 983040 | tf_op jit(solution)/shard_map/all_gather | solution.py:73
  238.7 0.7 bitcast_reduce_fusion
  239.4 0.5 fusion.29
  239.9 1.4 copy-done.1
  241.3 2.7 fusion
  244.0 0.0 reduce-scatter.5.cloned.1.call-update
  244.0 32.5 %reduce-scatter.5.cloned.1.call-done = f32[48,3200]{1,0:T(8,128)} async-done(((f32[192,3200]{1,0:T(8,128)}), f32[48,3200]{1,0:T(8,128)}) %reduce-scatter.5.cloned.1.call-update) | async-done | bytes 614416 | tf_op jit(solution)/shard_map/reduce_scatter | solution.py:86
  276.5 1.2 fusion.42
  277.7 1.9 maximum_bitcast_fusion
  (29 shorter events, 0.1 us)
Async XLA Ops:
  6.5 63.7 %copy-start = (bf16[1,3200,512]{2,1,0:T(8,128)(2,1)S(1)}, bf16[1,3200,512]{2,1,0:T(8,128)(2,1)}, u32[]{:S(2)}) copy-start(bf16[1,3200,512]{2,1,0:T(8,128)(2,1)} %param.16) | copy-start | bytes 9830404
  6.5 25.4 %all-gather.5.cloned.1.call-start = ((), (), s32[]{:S(2)}) async-start(), calls=%async_computation.2 | async-start | bytes 1536000 | tf_op jit(solution)/shard_map/all_gather | solution.py:36
  11.2 108.5 %all-gather.9.cloned.1.call-start = ((), (), s32[]{:S(2)}) async-start(), calls=%async_computation.6 | async-start | bytes 4096000 | tf_op jit(solution)/shard_map/all_gather | solution.py:83
  12.0 145.2 %reduce-scatter.3.cloned.1.call-start = ((), (), s32[]{:S(2)}) async-start(), calls=%async_computation.3 | async-start | bytes 3072000 | tf_op jit(solution)/shard_map/reduce_scatter | solution.py:86
  31.9 3.7 %copy-start.8 = (f32[1,128]{1,0:T(1,128)S(1)}, f32[1,128]{1,0:T(1,128)}, u32[]{:S(2)}) copy-start(f32[1,128]{1,0:T(1,128)} %param.13) | copy-start | bytes 1540
  66.4 3.8 %copy-start.10 = (bf16[192,3200]{1,0:T(8,128)(2,1)S(1)}, bf16[192,3200]{1,0:T(8,128)(2,1)}, u32[]{:S(2)}) copy-start(bf16[192,3200]{1,0:T(8,128)(2,1)} %all-gather.5.cloned.1.call-done) | copy-start | bytes 3686404
  70.3 31.3 %copy-start.3 = (bf16[768,512]{0,1:T(8,128)(2,1)S(1)}, bf16[768,512]{0,1:T(8,128)(2,1)}, u32[]{:S(2)}) copy-start(bf16[768,512]{0,1:T(8,128)(2,1)} %copy.18) | copy-start | bytes 2359300
  70.3 31.3 %copy-start.9 = (f32[1,128]{1,0:T(1,128)S(1)}, f32[1,128]{1,0:T(1,128)}, u32[]{:S(2)}) copy-start(f32[1,128]{1,0:T(1,128)} %param.12) | copy-start | bytes 1540
  124.3 65.7 %all-gather.7.cloned.1.call-start = ((), (), s32[]{:S(2)}) async-start(), calls=%async_computation.4 | async-start | bytes 1536000 | tf_op jit(solution)/shard_map/all_gather | solution.py:36
  158.4 3.4 %copy-start.6 = (bf16[48,3200]{1,0:T(8,128)(2,1)}, bf16[48,3200]{1,0:T(8,128)(2,1)S(1)}, u32[]{:S(2)}) copy-start(bf16[48,3200]{1,0:T(8,128)(2,1)S(1)} %fusion.37) | copy-start | bytes 921604
  158.4 9.9 %collective-permute-start = (bf16[48,3200]{1,0:T(8,128)(2,1)S(1)}, bf16[48,3200]{1,0:T(8,128)(2,1)S(1)}, u32[]{:S(2)}, u32[]{:S(2)}) collective-permute-start(bf16[48,3200]{1,0:T(8,128)(2,1)S(1)} %fusion.37), channel_id=1, source_target_pairs={{0,4},{1,5},{2,6},{3,7},{8,12},{9,13},{10,14},{11,15},{16,20},{17,... | collective-permute-start | bytes 921608 | tf_op jit(solution)/shard_map/ppermute | solution.py:13
  169.5 0.7 copy-start.5
  171.1 105.4 %reduce-scatter.5.cloned.1.call-start = ((), (), s32[]{:S(2)}) async-start(), calls=%async_computation.5 | async-start | bytes 3072000 | tf_op jit(solution)/shard_map/reduce_scatter | solution.py:86
  190.0 4.4 %copy-start.2 = (bf16[512,3200]{1,0:T(8,128)(2,1)S(1)}, bf16[512,3200]{1,0:T(8,128)(2,1)}, u32[]{:S(2)}) copy-start(bf16[512,3200]{1,0:T(8,128)(2,1)} %copy.32) | copy-start | bytes 9830404
  190.0 4.4 %copy-start.11 = (bf16[192,3200]{1,0:T(8,128)(2,1)S(1)}, bf16[192,3200]{1,0:T(8,128)(2,1)}, u32[]{:S(2)}) copy-start(bf16[192,3200]{1,0:T(8,128)(2,1)} %all-gather.7.cloned.1.call-done) | copy-start | bytes 3686404
  218.3 20.4 %copy-start.4 = (bf16[768,512]{0,1:T(8,128)(2,1)S(1)}, bf16[768,512]{0,1:T(8,128)(2,1)}, u32[]{:S(2)}) copy-start(bf16[768,512]{0,1:T(8,128)(2,1)} %copy.25) | copy-start | bytes 2359300
  218.3 20.4 %copy-start.7 = (f32[192,4,128]{2,0,1:T(8,128)S(1)}, f32[192,4,128]{2,0,1:T(8,128)}, u32[]{:S(2)}) copy-start(f32[192,4,128]{2,0,1:T(8,128)} %get-tuple-element.18) | copy-start | bytes 1179652
  239.4 1.9 copy-start.1
Sparse Core Ops, SparseCore 0:
  11.3 20.5 all-gather.4
  33.5 86.1 all-gather.8
  124.4 32.7 reduce-scatter.2
  171.2 18.7 all-gather.6
  244.1 32.2 reduce-scatter.4
where the time goes:
time: 287 us; the launch traced here: 286 us
  waiting for transfers between devices  117 us (41%)
  blocking collectives  96.9 us (34%)
  matrix products  26 us (9%)
  local copies, waits for them, and re-layouts  18.2 us (6%)
  between operations  13.3 us (5%)
  other arithmetic  11.3 us (4%)
  starting transfers between devices  3.54 us (1%)
    reduce_scatter x2, waiting for transfers between devices, per_device(): lax.psum_scatter(partial_value, 'mp', scatter_dimension=0, tiled=True)  65.3 us
    all_gather x2, blocking collectives, per_device(): lax.all_gather(projected[2], 'ctx', axis=0, tiled=True)  48.6 us
    all_gather x2, blocking collectives, per_device(): key_block = lax.all_gather(projected[1], 'ctx', axis=0, tiled=True)  48.3 us
    all_gather x2, waiting for transfers between devices, per_device(): project_segment = lax.all_gather(normed, 'mp', axis=0, tiled=True)  27.3 us
    all_gather x1, waiting for transfers between devices, per_device(): lax.all_gather(o_weight[0], 'ctx', axis=1, tiled=True)  16.9 us
    dot_general x2, matrix products, per_device(): jnp.dot(project_segment, q_weight[0], preferred_element_type=jnp.float32)  8.21 us
    dot_general x2, matrix products, per_device(): jnp.dot(attended, lax.all_gather(o_weight[0], 'ctx', axis=1, tiled=True),...  7.24 us
    ppermute x1, waiting for transfers between devices, shifted(): lax.ppermute(value, axis, [(source, source + steps) for source in range(l...  6.49 us
  transfers between devices with their start and end apart: 6, of which 6 were waited for; matrix products, arithmetic and copies ran while one was open for 8% of the time, Pallas kernels for 0%

commit v1 on v0

--- a/solution.py
+++ b/solution.py
@@ -33,7 +33,14 @@
         layer_input = jnp.where(section_index == 0, patches[micro_step], incoming)
         residual = layer_input.astype(jnp.float32)
         normed = rms_scaled(residual, layer_gain).astype(jnp.bfloat16)
-        project_segment = lax.all_gather(normed, "mp", axis=0, tiled=True)
+        ring = [normed]
+        for hop in range(3):
+            ring.append(lax.ppermute(ring[-1], "mp", [(dev, (dev + 1) % 4) for dev in range(4)]))
+        project_segment = jnp.roll(
+            jnp.concatenate(ring[::-1], axis=0),
+            (lax.axis_index("mp") + 1) * ring[0].shape[0],
+            axis=0,
+        )
         project_count = project_segment.shape[0]
         raw_query = jnp.dot(project_segment, q_weight[0], preferred_element_type=jnp.float32)
         raw_key = jnp.dot(project_segment, k_weight[0], preferred_element_type=jnp.float32)

time: 287 us -> 275 us (0.958)
  waiting for transfers between devices: 117 us -> 107 us
  blocking collectives: 96.9 us -> 88.1 us
  other arithmetic: 11.3 us -> 19.2 us
    ppermute x0 -> x6, waiting for transfers between devices: none -> 31.7 us  [per_device(): lax.ppermute(ring[-1], 'mp', [(dev, (dev + 1) % 4) for dev in range(4)])]
    all_gather x2 -> x0, waiting for transfers between devices: 27.3 us -> none  [per_device(): project_segment = lax.all_gather(normed, 'mp', axis=0, tiled=True)]
    all_gather x1, waiting for transfers between devices: 16.9 us -> 0.02 us  [per_device(): lax.all_gather(o_weight[0], 'ctx', axis=1, tiled=True)]
    all_gather x2, blocking collectives: 48.6 us -> 38.1 us  [per_device(): lax.all_gather(projected[2], 'ctx', axis=0, tiled=True)]
    concatenate x0 -> x2, other arithmetic: none -> 9.16 us  [per_device(): jnp.roll(jnp.concatenate(ring[::-1], axis=0), (lax.axis_index('mp') + 1)...]
  transfers between devices with their start and end apart: 6 -> 10, of which waited for: 6 -> 8; matrix products, arithmetic and copies ran while one was open for 8% -> 12% of each run, Pallas kernels for 0% -> 0%
where the time goes in v1:
time: 275 us
  waiting for transfers between devices  107 us (39%)
  blocking collectives  88.1 us (32%)
  matrix products  23.5 us (9%)
  local copies, waits for them, and re-layouts  19.5 us (7%)
  other arithmetic  19.2 us (7%)
  between operations  13.4 us (5%)
  starting transfers between devices  3.97 us (1%)
    reduce_scatter x2, waiting for transfers between devices, per_device(): lax.psum_scatter(partial_value, 'mp', scatter_dimension=0, tiled=True)  68 us
    all_gather x2, blocking collectives, per_device(): key_block = lax.all_gather(projected[1], 'ctx', axis=0, tiled=True)  50 us
    all_gather x2, blocking collectives, per_device(): lax.all_gather(projected[2], 'ctx', axis=0, tiled=True)  38.1 us
    ppermute x6, waiting for transfers between devices, per_device(): lax.ppermute(ring[-1], 'mp', [(dev, (dev + 1) % 4) for dev in range(4)])  31.7 us
    concatenate x2, other arithmetic, per_device(): jnp.roll(jnp.concatenate(ring[::-1], axis=0), (lax.axis_index('mp') + 1)...  9.16 us
    dot_general x2, matrix products, per_device(): jnp.dot(attended, lax.all_gather(o_weight[0], 'ctx', axis=1, tiled=True),...  7.22 us
    ppermute x1, waiting for transfers between devices, shifted(): lax.ppermute(value, axis, [(source, source + steps) for source in range(l...  6.49 us
    dot_general x2, matrix products, per_device(): jnp.dot(project_segment, q_weight[0], preferred_element_type=jnp.float32)  5.74 us
  transfers between devices with their start and end apart: 10, of which 8 were waited for; matrix products, arithmetic and copies ran while one was open for 12% of the time, Pallas kernels for 0%

profile of v1, /device:TPU:0, one launch (start us, length us, event | category | flops | bytes accessed | tf_op | source)
XLA Modules:
  0.0 274.7 jit_solution(5258328181586461680)
XLA Ops:
  6.5 0.7 all-gather.3.cloned.1.call-update
  7.3 2.1 fusion.48
  9.4 0.8 reduce
  10.2 1.1 fusion.50
  11.3 0.7 copy-done.9
  12.0 0.5 collective-permute-start
  12.5 6.5 %collective-permute-done = bf16[48,3200]{1,0:T(8,128)(2,1)S(1)} collective-permute-done((bf16[48,3200]{1,0:T(8,128)(2,1)S(1)}, bf16[48,3200]{1,0:T(8,128)(2,1)S(1)}, u32[]{:S(2)}, u32[]{:S(2)}) %collective-permute-start) | collective-permute-done | bytes 307232 | tf_op jit(solution)/shard_map/ppermute | solution.py:38
  19.0 0.7 copy-done.10
  19.7 6.4 %collective-permute-done.1 = bf16[48,3200]{1,0:T(8,128)(2,1)} collective-permute-done((bf16[48,3200]{1,0:T(8,128)(2,1)S(1)}, bf16[48,3200]{1,0:T(8,128)(2,1)}, u32[]{:S(2)}, u32[]{:S(2)}) %collective-permute-start.1) | collective-permute-done | bytes 307232 | tf_op jit(solution)/shard_map/ppermute | solution.py:38
  26.1 5.7 %copy.32 = bf16[512,3200]{1,0:T(8,128)(2,1)} copy(bf16[512,3200]{0,1:T(8,128)(2,1)} %bitcast.129) | data formatting | bytes 6553600 | tf_op jit(solution)/shard_map/dot_general | solution.py:46
  31.8 5.7 %copy.33 = bf16[512,3200]{1,0:T(8,128)(2,1)} copy(bf16[512,3200]{0,1:T(8,128)(2,1)} %bitcast.130) | data formatting | bytes 6553600 | tf_op jit(solution)/shard_map/dot_general | solution.py:45
  37.4 4.9 %fusion.18 = bf16[192,3200]{1,0:T(8,128)(2,1)S(1)} fusion(s32[]{:T(128)S(6)} %select_n.28, bf16[48,3200]{1,0:T(8,128)(2,1)} %collective-permute-done.2, bf16[48,3200]{1,0:T(8,128)(2,1)} %collective-permute-done.1, bf16[48,3200]{1,0:T(8,128)(2,1)} %copy-done.10, bf16[48,3200]{1,0:T(8,128)(2,1)} %copy-done.9), kind=kLoop, calls=%fused_computation.40 | loop fusion | flops 9830400 | bytes 2457604 | tf_op jit(solution)/shard_map/jit(_roll_dynamic)/concatenate | solution.py:39
  42.3 3.8 %multiply_reduce_fusion.3 = (f32[192,4]{0,1:T(4,128)S(1)}, f32[192,4,128]{2,0,1:T(8,128)S(1)}) fusion(bf16[4,128,3200]{2,1,0:T(8,128)(2,1)} %bitcast.131, bf16[192,3200]{1,0:T(8,128)(2,1)S(1)} %fusion.18), kind=kOutput, calls=%fused_computation.90 | convolution fusion | flops 629341440 | bytes 4901888 | tf_op jit(solution)/shard_map/dot_general | solution.py:46
  46.2 0.2 copy_bitcast_fusion.1
  46.3 31.2 %all_gather.17 = bf16[768,512]{1,0:T(8,128)(2,1)} all-gather(bf16[192,512]{1,0:T(8,128)(2,1)S(1)} %copy_bitcast_fusion.1), channel_id=1, replica_groups=mesh['ctx'=4,'section'=2,'mp'=4] {'ctx'}, dimensions={0}, use_global_device_ids=true | all-gather | bytes 983040 | tf_op jit(solution)/shard_map/all_gather | solution.py:64
  77.5 2.3 copy.18
  79.8 3.8 %multiply_reduce_fusion.2 = (f32[192,4]{0,1:T(4,128)S(1)}, f32[192,4,128]{2,0,1:T(8,128)S(1)}) fusion(bf16[4,128,3200]{2,1,0:T(8,128)(2,1)} %bitcast.133, bf16[192,3200]{1,0:T(8,128)(2,1)} %copy-done.6), kind=kOutput, calls=%fused_computation.88 | convolution fusion | flops 629341440 | bytes 4901888 | tf_op jit(solution)/shard_map/dot_general | solution.py:45
  83.6 0.8 fusion.36
  84.5 20.6 %all_gather.16 = bf16[768,512]{1,0:T(8,128)(2,1)S(1)} all-gather(bf16[192,512]{1,0:T(8,128)(2,1)S(1)} %fusion.36), channel_id=1, replica_groups=mesh['ctx'=4,'section'=2,'mp'=4] {'ctx'}, dimensions={0}, use_global_device_ids=true | all-gather | bytes 983040 | tf_op jit(solution)/shard_map/all_gather | solution.py:80
  105.1 0.7 bitcast_reduce_fusion.1
  105.8 0.5 fusion.42
  106.3 4.6 %fusion.2 = f32[192,3200]{1,0:T(8,128)} fusion(bf16[1,512,3200]{1,2,0:T(8,128)(2,1)} %all-gather.3.cloned.1.call-done, bf16[4,24,8,128]{3,2,1,0:T(8,128)(2,1)S(1)} %fusion.42), kind=kOutput, calls=%fused_computation.2 | convolution fusion | flops 629145600 | bytes 5931008 | tf_op jit(solution)/shard_map/dot_general | solution.py:88
  111.0 33.6 %reduce-scatter.3.cloned.1.call-done = f32[48,3200]{1,0:T(8,128)} async-done(((f32[192,3200]{1,0:T(8,128)}), f32[48,3200]{1,0:T(8,128)}) %reduce-scatter.3.cloned.1.call-update) | async-done | bytes 614416 | tf_op jit(solution)/shard_map/reduce_scatter | solution.py:93
  144.6 1.4 fusion.51
  145.9 3.4 %collective-permute-start.3 = (bf16[48,3200]{1,0:T(8,128)(2,1)S(1)}, bf16[48,3200]{1,0:T(8,128)(2,1)S(1)}, u32[]{:S(2)}, u32[]{:S(2)}) collective-permute-start(bf16[48,3200]{1,0:T(8,128)(2,1)S(1)} %fusion.51), channel_id=1, source_target_pairs={{0,4},{1,5},{2,6},{3,7},{8,12},{9,13},{10,14},{11,15},{16,20},{17,... | collective-permute-start | bytes 921608 | tf_op jit(solution)/shard_map/ppermute | solution.py:13
  149.3 6.5 %collective-permute-done.3 = bf16[48,3200]{1,0:T(8,128)(2,1)S(1)} collective-permute-done((bf16[48,3200]{1,0:T(8,128)(2,1)S(1)}, bf16[48,3200]{1,0:T(8,128)(2,1)S(1)}, u32[]{:S(2)}, u32[]{:S(2)}) %collective-permute-start.3) | collective-permute-done | bytes 307232 | tf_op jit(solution)/shard_map/ppermute | solution.py:13
  155.8 1.2 fusion.52
  157.0 0.7 copy-done.5
  157.7 0.1 fusion.54
  157.9 0.1 collective-permute-start.4
  157.9 6.3 %collective-permute-done.4 = bf16[48,3200]{1,0:T(8,128)(2,1)S(1)} collective-permute-done((bf16[48,3200]{1,0:T(8,128)(2,1)S(1)}, bf16[48,3200]{1,0:T(8,128)(2,1)S(1)}, u32[]{:S(2)}, u32[]{:S(2)}) %collective-permute-start.4) | collective-permute-done | bytes 307232 | tf_op jit(solution)/shard_map/ppermute | solution.py:38
  164.2 6.3 %collective-permute-done.5 = bf16[48,3200]{1,0:T(8,128)(2,1)S(1)} collective-permute-done((bf16[48,3200]{1,0:T(8,128)(2,1)S(1)}, bf16[48,3200]{1,0:T(8,128)(2,1)S(1)}, u32[]{:S(2)}, u32[]{:S(2)}) %collective-permute-start.5) | collective-permute-done | bytes 307232 | tf_op jit(solution)/shard_map/ppermute | solution.py:38
  170.5 6.3 %collective-permute-done.6 = bf16[48,3200]{1,0:T(8,128)(2,1)S(1)} collective-permute-done((bf16[48,3200]{1,0:T(8,128)(2,1)S(1)}, bf16[48,3200]{1,0:T(8,128)(2,1)S(1)}, u32[]{:S(2)}, u32[]{:S(2)}) %collective-permute-start.6) | collective-permute-done | bytes 307232 | tf_op jit(solution)/shard_map/ppermute | solution.py:38
  176.8 4.3 %fusion.11 = bf16[192,3200]{1,0:T(8,128)(2,1)S(1)} fusion(s32[]{:T(128)S(6)} %select_n.28, bf16[48,3200]{1,0:T(8,128)(2,1)S(1)} %collective-permute-done.6, bf16[48,3200]{1,0:T(8,128)(2,1)S(1)} %collective-permute-done.5, bf16[48,3200]{1,0:T(8,128)(2,1)S(1)} %collective-permute-done.4, bf16[48,3200]{1,0:T(8,128)(2,1)S(1)} %fusion.54), kind=kLoop, calls=%fused_computation.33 | loop fusion | flops 9830400 | bytes 2457604 | tf_op jit(solution)/shard_map/jit(_roll_dynamic)/concatenate | solution.py:39
  181.1 2.0 multiply_reduce_fusion
  183.0 1.4 multiply_reduce_fusion.1
  184.4 0.8 fusion.39
  185.3 0.2 copy_bitcast_fusion
  185.5 18.8 %all_gather.20 = bf16[768,512]{1,0:T(8,128)(2,1)} all-gather(bf16[192,512]{1,0:T(8,128)(2,1)S(1)} %copy_bitcast_fusion), channel_id=1, replica_groups=mesh['ctx'=4,'section'=2,'mp'=4] {'ctx'}, dimensions={0}, use_global_device_ids=true | all-gather | bytes 983040 | tf_op jit(solution)/shard_map/all_gather | solution.py:64
  204.3 2.3 copy.25
  206.6 17.5 %all_gather.19 = bf16[768,512]{1,0:T(8,128)(2,1)S(1)} all-gather(bf16[192,512]{1,0:T(8,128)(2,1)S(1)} %fusion.39), channel_id=1, replica_groups=mesh['ctx'=4,'section'=2,'mp'=4] {'ctx'}, dimensions={0}, use_global_device_ids=true | all-gather | bytes 983040 | tf_op jit(solution)/shard_map/all_gather | solution.py:80
  224.1 1.9 bitcast_reduce_fusion
  226.1 0.5 fusion.43
  226.6 1.4 copy-done.1
  228.0 2.7 fusion
  230.7 34.4 %reduce-scatter.5.cloned.1.call-done = f32[48,3200]{1,0:T(8,128)} async-done(((f32[192,3200]{1,0:T(8,128)}), f32[48,3200]{1,0:T(8,128)}) %reduce-scatter.5.cloned.1.call-update) | async-done | bytes 614416 | tf_op jit(solution)/shard_map/reduce_scatter | solution.py:93
  265.1 1.2 fusion.56
  266.3 1.9 maximum_bitcast_fusion
  (39 shorter events, 0.2 us)
Async XLA Ops:
  6.5 77.1 %copy-start = (bf16[1,3200,512]{2,1,0:T(8,128)(2,1)S(1)}, bf16[1,3200,512]{2,1,0:T(8,128)(2,1)}, u32[]{:S(2)}) copy-start(bf16[1,3200,512]{2,1,0:T(8,128)(2,1)} %param.18) | copy-start | bytes 9830404
  6.5 99.8 %all-gather.3.cloned.1.call-start = ((), (), s32[]{:S(2)}) async-start(), calls=%async_computation.4 | async-start | bytes 4096000 | tf_op jit(solution)/shard_map/all_gather | solution.py:90
  7.3 137.3 %reduce-scatter.3.cloned.1.call-start = ((), (), s32[]{:S(2)}) async-start(), calls=%async_computation.2 | async-start | bytes 3072000 | tf_op jit(solution)/shard_map/reduce_scatter | solution.py:93
  11.3 0.7 copy-start.9
  12.0 6.9 %collective-permute-start = (bf16[48,3200]{1,0:T(8,128)(2,1)S(1)}, bf16[48,3200]{1,0:T(8,128)(2,1)S(1)}, u32[]{:S(2)}, u32[]{:S(2)}) collective-permute-start(bf16[48,3200]{1,0:T(8,128)(2,1)S(1)} %fusion.50), channel_id=1, source_target_pairs={{0,1},{1,2},{2,3},{3,0},{4,5},{5,6},{6,7},{7,4},{8,9},{9,10},{10,1... | collective-permute-start | bytes 921608 | tf_op jit(solution)/shard_map/ppermute | solution.py:38
  19.0 0.7 copy-start.10
  19.7 6.4 %collective-permute-start.1 = (bf16[48,3200]{1,0:T(8,128)(2,1)S(1)}, bf16[48,3200]{1,0:T(8,128)(2,1)}, u32[]{:S(2)}, u32[]{:S(2)}) collective-permute-start(bf16[48,3200]{1,0:T(8,128)(2,1)S(1)} %collective-permute-done), channel_id=1, source_target_pairs={{0,1},{1,2},{2,3},{3,0},{4,5},{5,6},{6,7},{7,4},{8,9},{9,10},{10,1... | collective-permute-start | bytes 921608 | tf_op jit(solution)/shard_map/ppermute | solution.py:38
  26.1 11.3 %collective-permute-start.2 = (bf16[48,3200]{1,0:T(8,128)(2,1)}, bf16[48,3200]{1,0:T(8,128)(2,1)}, u32[]{:S(2)}, u32[]{:S(2)}) collective-permute-start(bf16[48,3200]{1,0:T(8,128)(2,1)} %collective-permute-done.1), channel_id=1, source_target_pairs={{0,1},{1,2},{2,3},{3,0},{4,5},{5,6},{6,7},{7,4},{8,9},{9,10},{10,1... | collective-permute-start | bytes 921608 | tf_op jit(solution)/shard_map/ppermute | solution.py:38
  42.3 3.8 %copy-start.6 = (bf16[192,3200]{1,0:T(8,128)(2,1)}, bf16[192,3200]{1,0:T(8,128)(2,1)S(1)}, u32[]{:S(2)}) copy-start(bf16[192,3200]{1,0:T(8,128)(2,1)S(1)} %fusion.18) | copy-start | bytes 3686404
  42.3 3.8 %copy-start.11 = (f32[1,128]{1,0:T(1,128)S(1)}, f32[1,128]{1,0:T(1,128)}, u32[]{:S(2)}) copy-start(f32[1,128]{1,0:T(1,128)} %param.15) | copy-start | bytes 1540
  79.8 3.8 %copy-start.7 = (bf16[192,3200]{1,0:T(8,128)(2,1)S(1)}, bf16[192,3200]{1,0:T(8,128)(2,1)}, u32[]{:S(2)}) copy-start(bf16[192,3200]{1,0:T(8,128)(2,1)} %copy-done.6) | copy-start | bytes 3686404
  83.6 21.4 %copy-start.4 = (bf16[768,512]{0,1:T(8,128)(2,1)S(1)}, bf16[768,512]{0,1:T(8,128)(2,1)}, u32[]{:S(2)}) copy-start(bf16[768,512]{0,1:T(8,128)(2,1)} %copy.18) | copy-start | bytes 2359300
  83.6 21.4 %copy-start.12 = (f32[1,128]{1,0:T(1,128)S(1)}, f32[1,128]{1,0:T(1,128)}, u32[]{:S(2)}) copy-start(f32[1,128]{1,0:T(1,128)} %param.14) | copy-start | bytes 1540
  110.9 154.1 %reduce-scatter.5.cloned.1.call-start = ((), (), s32[]{:S(2)}) async-start(), calls=%async_computation.3 | async-start | bytes 3072000 | tf_op jit(solution)/shard_map/reduce_scatter | solution.py:93
  144.6 36.5 %copy-start.3 = (bf16[512,3200]{1,0:T(8,128)(2,1)S(1)}, bf16[512,3200]{1,0:T(8,128)(2,1)}, u32[]{:S(2)}) copy-start(bf16[512,3200]{1,0:T(8,128)(2,1)} %copy.33) | copy-start | bytes 9830404
  145.9 3.4 %copy-start.8 = (bf16[48,3200]{1,0:T(8,128)(2,1)}, bf16[48,3200]{1,0:T(8,128)(2,1)S(1)}, u32[]{:S(2)}) copy-start(bf16[48,3200]{1,0:T(8,128)(2,1)S(1)} %fusion.51) | copy-start | bytes 921604
  145.9 9.9 %collective-permute-start.3 = (bf16[48,3200]{1,0:T(8,128)(2,1)S(1)}, bf16[48,3200]{1,0:T(8,128)(2,1)S(1)}, u32[]{:S(2)}, u32[]{:S(2)}) collective-permute-start(bf16[48,3200]{1,0:T(8,128)(2,1)S(1)} %fusion.51), channel_id=1, source_target_pairs={{0,4},{1,5},{2,6},{3,7},{8,12},{9,13},{10,14},{11,15},{16,20},{17,... | collective-permute-start | bytes 921608 | tf_op jit(solution)/shard_map/ppermute | solution.py:13
  157.0 0.7 copy-start.5
  157.9 6.3 %collective-permute-start.4 = (bf16[48,3200]{1,0:T(8,128)(2,1)S(1)}, bf16[48,3200]{1,0:T(8,128)(2,1)S(1)}, u32[]{:S(2)}, u32[]{:S(2)}) collective-permute-start(bf16[48,3200]{1,0:T(8,128)(2,1)S(1)} %fusion.54), channel_id=1, source_target_pairs={{0,1},{1,2},{2,3},{3,0},{4,5},{5,6},{6,7},{7,4},{8,9},{9,10},{10,1... | collective-permute-start | bytes 921608 | tf_op jit(solution)/shard_map/ppermute | solution.py:38
  164.2 6.3 %collective-permute-start.5 = (bf16[48,3200]{1,0:T(8,128)(2,1)S(1)}, bf16[48,3200]{1,0:T(8,128)(2,1)S(1)}, u32[]{:S(2)}, u32[]{:S(2)}) collective-permute-start(bf16[48,3200]{1,0:T(8,128)(2,1)S(1)} %collective-permute-done.4), channel_id=1, source_target_pairs={{0,1},{1,2},{2,3},{3,0},{4,5},{5,6},{6,7},{7,4},{8,9},{9,10},{10,1... | collective-permute-start | bytes 921608 | tf_op jit(solution)/shard_map/ppermute | solution.py:38
  170.5 6.3 %collective-permute-start.6 = (bf16[48,3200]{1,0:T(8,128)(2,1)S(1)}, bf16[48,3200]{1,0:T(8,128)(2,1)S(1)}, u32[]{:S(2)}, u32[]{:S(2)}) collective-permute-start(bf16[48,3200]{1,0:T(8,128)(2,1)S(1)} %collective-permute-done.5), channel_id=1, source_target_pairs={{0,1},{1,2},{2,3},{3,0},{4,5},{5,6},{6,7},{7,4},{8,9},{9,10},{10,1... | collective-permute-start | bytes 921608 | tf_op jit(solution)/shard_map/ppermute | solution.py:38
  181.1 2.0 copy-start.2
  226.1 1.9 copy-start.1
Sparse Core Ops, SparseCore 0:
  8.9 80.8 all-gather.2
  111.0 33.4 reduce-scatter.2
  230.8 34.2 reduce-scatter.4
